TPU v7x, 512 devices: a whole 4x8x8 slice. The times are simulated.
512 devices in a mesh: member: 32 (over z, x), wave: 16 (over y, core).
Axes of the slice: x: 4, y: 8, z: 8, core: 2. Of those that a mesh axis runs over, the one named last changes fastest.
Arguments:
- state: float32 [32, 128, 32, 640], P('member', 'wave'), may hold values from -6 to 6
- legendre: bfloat16 [128, 640, 640], P('wave'), may hold values from -0.25 to 0.25
- lat_weights: float32 [640], replicated, may hold values from 0.5 to 2
- region: int32 [4], replicated, may hold values from 0 to 2560, as said below
- sources: int32 [32], replicated, may hold values from 0 to 31, as said below
Outputs:
- new_states: float32 [32, 128, 32, 640], P('member', 'wave')
- scores: float32 [32], P('member')
Inputs may be any that keep to these rules, and one draw needn't show every extreme that they name: region[0] < region[1] bound the latitudes and region[2] < region[3] the longitudes of the region; each band covers at least half of its grid dimension; the longitude band ends at the last longitude, region[3] = 2560. `sources`: some member is the source of at least 8 slots.
All inputs are finite; a program needn't handle non-finite values.
Results may differ from a plain program's by a relative error of at most 0.0059.
Values may be sent and summed in bfloat16 or wider, within the bound.
No kernel may reach another device: no remote copies, remote signals or barrier semaphores. Data moves between devices by JAX's collectives and lax.ppermute only.
A program may use at most 128 MiB of HBM per device.

v0:
```python
import jax
import jax.numpy as jnp
from jax import lax
from jax.sharding import PartitionSpec as P

NLON = 2560
advect_rate = 2.0


def fourier_table(waves_total, points):
    wave_index = lax.broadcasted_iota(jnp.int32, (waves_total, points), 0)
    column_index = lax.broadcasted_iota(jnp.int32, (waves_total, points), 1)
    angles = (wave_index * column_index % points).astype(jnp.float32) * (2.0 * jnp.pi / points)
    return jnp.stack([jnp.cos(angles), -jnp.sin(angles)], axis=1).astype(jnp.bfloat16)


def on_device(state, legendre, lat_weights, region, sources):
    wave_count = lax.axis_size("wave")
    waves_local = legendre.shape[0]
    waves_total = waves_local * wave_count
    degrees = legendre.shape[1]
    latitudes = legendre.shape[2]
    lat_rows = latitudes // wave_count
    state_rows = state.shape[2]
    level_count = state_rows // 4
    fourier = fourier_table(waves_total, NLON)
    spectral = state[0]
    fourier_coef = jnp.einsum(
        "mrn,mnl->mrl", spectral.astype(jnp.bfloat16), legendre, preferred_element_type=jnp.float32
    )
    fourier_coef = fourier_coef.astype(jnp.bfloat16).reshape(
        waves_local, 2, 2 * level_count, latitudes
    )
    synthesis_scale = (2.0 * waves_total) ** (-0.5)
    gridded = synthesis_scale * jnp.einsum(
        "mckl,mcx->klx",
        lax.all_to_all(fourier_coef, "wave", split_axis=3, concat_axis=0, tiled=True),
        fourier,
        preferred_element_type=jnp.float32,
    )
    lat_start = lax.axis_index("wave") * lat_rows
    local_weights = lax.dynamic_slice_in_dim(lat_weights, lat_start, lat_rows)
    wind_grid = gridded[:level_count]
    temper_grid = gridded[level_count:]
    fluxes = (
        jnp.concatenate([0.5 * wind_grid * wind_grid, wind_grid * temper_grid], axis=0)
        * local_weights[None, :, None]
    )
    fluxes = fluxes.astype(jnp.bfloat16)
    lat_index = lat_start + lax.broadcasted_iota(jnp.int32, (lat_rows, 1), 0)
    lon_index = lax.broadcasted_iota(jnp.int32, (1, NLON), 1)
    in_region = (
        (lat_index >= region[0])
        & (lat_index < region[1])
        & (lon_index >= region[2])
        & (lon_index < region[3])
    )
    lowest = temper_grid[level_count - 1]
    region_part = jnp.sum(jnp.where(in_region, local_weights[:, None] * lowest * lowest, 0.0))
    region_total = lax.psum(region_part, "wave")
    every_lat = lax.broadcasted_iota(jnp.int32, (latitudes,), 0)
    lat_inside = (every_lat >= region[0]) & (every_lat < region[1])
    region_weight = jnp.sum(jnp.where(lat_inside, lat_weights, 0.0)) * (
        region[3] - region[2]
    ).astype(jnp.float32)
    scores = (region_total / region_weight).reshape(1)
    analysis_scale = NLON ** (-0.5)
    flux_coef = analysis_scale * jnp.einsum(
        "klx,mcx->mckl", fluxes, fourier, preferred_element_type=jnp.float32
    )
    flux_coef = flux_coef.astype(jnp.bfloat16)
    tendency = jnp.einsum(
        "mckl,mnl->mckn",
        lax.all_to_all(flux_coef, "wave", split_axis=0, concat_axis=3, tiled=True),
        legendre,
        preferred_element_type=jnp.float32,
    )
    wave_ids = lax.axis_index("wave") * waves_local + lax.broadcasted_iota(
        jnp.int32, (waves_local, 1, 1), 0
    )
    advection = advect_rate * wave_ids.astype(jnp.float32) / waves_total
    degree_ids = lax.broadcasted_iota(jnp.int32, (1, 1, degrees), 2).astype(jnp.float32)
    damping = 1.0 + ((degree_ids + 1.0) / degrees) ** 2
    spectral_split = spectral.reshape(waves_local, 2, 2 * level_count, degrees)
    real_part = (spectral_split[:, 0] + advection * tendency[:, 1]) / damping
    imag_part = (spectral_split[:, 1] - advection * tendency[:, 0]) / damping
    stepped = jnp.stack([real_part, imag_part], axis=1).reshape(1, waves_local, state_rows, degrees)
    source_member = sources[lax.axis_index("member")]
    shards = lax.all_gather(stepped, "member", axis=0, tiled=True)
    owners = lax.broadcasted_iota(jnp.int32, (shards.shape[0], 1, 1, 1), 0)
    cloned = jnp.sum(jnp.where(owners == source_member, shards, 0.0), axis=0, keepdims=True)
    return (cloned, scores)


def solution(mesh):
    in_specs = (P("member", "wave", None, None), P("wave", None, None), P(), P(), P())
    out_specs = (P("member", "wave", None, None), P("member"))
    return jax.shard_map(
        on_device, mesh=mesh, in_specs=in_specs, out_specs=out_specs, check_vma=False
    )
```

profile of v0, /device:TPU:1, one launch (start us, length us, event | category | flops | bytes accessed | tf_op | source)
XLA Modules:
  0.0 273.9 jit_solution(7735756794780903431)
XLA Ops:
  7.2 4.2 %convolution_convert_fusion = bf16[8,32,640]{2,1,0:T(8,128)(2,1)S(1)} fusion(bf16[8,640,640]{2,1,0:T(8,128)(2,1)} %param.6, f32[1,8,32,640]{3,2,1,0:T(8,128)} %param.5), kind=kOutput, calls=%fused_computation.24 | convolution fusion | flops 210042880 | bytes 7536640 | tf_op jit(solution)/shard_map/mrn,mnl->mrl/dot_general | solution.py:28
  11.4 3.3 %copy.16 = bf16[8,2,16,640]{2,1,0,3:T(2,128)(2,1)S(1)} copy(bf16[8,2,16,640]{3,2,1,0:T(8,128)(2,1)S(1)} %bitcast.65) | data formatting | bytes 655360 | tf_op jit(solution)/shard_map/reshape | solution.py:31
  14.7 3.4 %reshape.118 = bf16[16,2,5120]{2,1,0:T(2,128)(2,1)} reshape(bf16[640,8,2,16]{3,2,1,0:T(2,128)(2,1)S(1)} %bitcast.60) | data formatting | bytes 655360
  18.1 10.8 %all-to-all-start = ((bf16[16,2,5120]{2,1,0:T(2,128)(2,1)}), bf16[16,2,5120]{2,1,0:T(2,128)(2,1)}, u32[]{:S(2)}, u32[]{:S(2)}) async-start(bf16[16,2,5120]{2,1,0:T(2,128)(2,1)} %reshape.118), calls=%async_computation | async-start | bytes 655360 | tf_op jit(solution)/shard_map/all_to_all | solution.py:37
  29.0 6.1 %negate_convert_fusion = (bf16[128,1,2560]{2,0,1:T(8,128)(2,1)S(1)}, bf16[128,1,2560]{2,0,1:T(8,128)(2,1)}) fusion(), kind=kLoop, calls=%fused_computation.16 | loop fusion | flops 3932160 | bytes 1310720 | tf_op jit(solution)/shard_map/convert.1
  35.2 6.3 %all-to-all-done = bf16[16,2,5120]{2,1,0:T(2,128)(2,1)} async-done(((bf16[16,2,5120]{2,1,0:T(2,128)(2,1)}), bf16[16,2,5120]{2,1,0:T(2,128)(2,1)}, u32[]{:S(2)}, u32[]{:S(2)}) %all-to-all-start) | async-done | bytes 327712 | tf_op jit(solution)/shard_map/all_to_all | solution.py:37
  41.4 8.5 %reshape.119 = bf16[640,8,2,16]{3,2,1,0:T(2,128)(2,1)S(1)} reshape(bf16[16,2,5120]{2,1,0:T(2,128)(2,1)} %all-to-all-done) | data formatting | bytes 655360
  50.0 4.7 %copy.27 = bf16[8,2,16,16,40]{4,0,3,1,2:T(8,128)(2,1)} copy(bf16[8,2,16,16,40]{2,1,0,4,3:T(2,128)(2,1)S(1)} %bitcast.61) | data formatting | bytes 655360 | tf_op jit(solution)/shard_map/all_to_all | solution.py:37
  54.7 2.5 bitcast_multiply_fusion
  57.2 0.8 multiply_multiply_fusion
  58.1 1.9 copy-done
  60.0 1.2 fusion.18
  61.2 1.4 copy.20
  62.6 2.4 reshape.120
  65.0 3.6 %all-to-all-start.1 = ((bf16[16,2,5120]{2,1,0:T(2,128)(2,1)}), bf16[16,2,5120]{2,1,0:T(2,128)(2,1)S(1)}, u32[]{:S(2)}, u32[]{:S(2)}) async-start(bf16[16,2,5120]{2,1,0:T(2,128)(2,1)} %reshape.120), calls=%async_computation.1 | async-start | bytes 655360 | tf_op jit(solution)/shard_map/all_to_all | solution.py:74
  68.7 0.3 all-gather.2.cloned.1.call-start
  69.0 12.8 %all-to-all-done.1 = bf16[16,2,5120]{2,1,0:T(2,128)(2,1)S(1)} async-done(((bf16[16,2,5120]{2,1,0:T(2,128)(2,1)}), bf16[16,2,5120]{2,1,0:T(2,128)(2,1)S(1)}, u32[]{:S(2)}, u32[]{:S(2)}) %all-to-all-start.1) | async-done | bytes 327712 | tf_op jit(solution)/shard_map/all_to_all | solution.py:74
  81.7 1.6 reshape.121
  83.4 0.7 copy.21
  84.1 1.2 all_to_all.33
  85.3 4.9 %fusion.1 = f32[8,2,16,640]{3,2,1,0:T(8,128)S(1)} fusion(bf16[8,2,16,640]{3,2,1,0:T(8,128)(2,1)S(1)} %all_to_all.33, bf16[8,640,640]{2,1,0:T(8,128)(2,1)} %param.6), kind=kOutput, calls=%fused_computation.3 | convolution fusion | flops 209715200 | bytes 7536640 | tf_op jit(solution)/shard_map/mckl,mnl->mckn/dot_general | solution.py:72
  90.4 0.9 pad_maximum_fusion.3
  91.4 0.7 fusion.36
  93.3 0.6 dynamic_slice.6
  93.9 0.6 iota_compare_fusion.4
  94.5 1.3 compare_and_fusion
  95.9 1.3 iota_compare_fusion
  97.1 1.9 select_reduce_fusion.1
  99.0 1.9 fusion.25
  101.5 23.4 %psum.7 = f32[]{:T(128)} all-reduce(f32[]{:T(128)} %fusion.25), channel_id=1, replica_groups=mesh['member'=32,'wave'=16] {'wave'}, use_global_device_ids=true, to_apply=%region_2.3 | all-reduce | flops 1 | bytes 8 | tf_op jit(solution)/shard_map/psum | solution.py:60
  125.5 130.8 %all-gather.2.cloned.1.call-done = f32[32,8,32,640]{3,2,1,0:T(8,128)} async-done(((f32[1,8,32,640]{3,2,1,0:T(8,128)}), f32[32,8,32,640]{3,2,1,0:T(8,128)}) %all-gather.2.cloned.1.call-update) | async-done | bytes 20971536 | tf_op jit(solution)/shard_map/all_gather | solution.py:89
  256.3 9.6 %select_reduce_fusion = f32[8,32,640]{2,1,0:T(8,128)} fusion(f32[32,8,32,640]{3,2,1,0:T(8,128)} %all-gather.2.cloned.1.call-done, pred[32]{0:T(512)(128)(4,1)S(1)} %iota_compare_fusion.4), kind=kLoop, calls=%fused_computation | loop fusion | flops 10321920 | bytes 21626912 | tf_op jit(solution)/shard_map/reduce_sum | solution.py:91
  (16 shorter events, 0.3 us)
Async XLA Ops:
  11.4 17.6 %copy-start.4 = (f32[640]{0:T(1024)S(1)}, f32[640]{0:T(1024)}, u32[]{:S(2)}) copy-start(f32[640]{0:T(1024)} %param.7) | copy-start | bytes 7684
  18.1 23.3 %all-to-all-start = ((bf16[16,2,5120]{2,1,0:T(2,128)(2,1)}), bf16[16,2,5120]{2,1,0:T(2,128)(2,1)}, u32[]{:S(2)}, u32[]{:S(2)}) async-start(bf16[16,2,5120]{2,1,0:T(2,128)(2,1)} %reshape.118), calls=%async_computation | async-start | bytes 655360 | tf_op jit(solution)/shard_map/all_to_all | solution.py:37
  57.2 2.8 %copy-start = (f32[16,40,2560]{2,1,0:T(8,128)}, f32[16,40,2560]{2,1,0:T(8,128)S(1)}, u32[]{:S(2)}) copy-start(f32[16,40,2560]{2,1,0:T(8,128)S(1)} %bitcast_multiply_fusion) | copy-start | bytes 19660804
  57.2 2.7 %copy-start.2 = (bf16[128,1,2560]{2,0,1:T(8,128)(2,1)S(1)}, bf16[128,1,2560]{2,0,1:T(8,128)(2,1)}, u32[]{:S(2)}) copy-start(bf16[128,1,2560]{2,0,1:T(8,128)(2,1)} %get-tuple-element.11) | copy-start | bytes 1966084
  65.0 16.7 %all-to-all-start.1 = ((bf16[16,2,5120]{2,1,0:T(2,128)(2,1)}), bf16[16,2,5120]{2,1,0:T(2,128)(2,1)S(1)}, u32[]{:S(2)}, u32[]{:S(2)}) async-start(bf16[16,2,5120]{2,1,0:T(2,128)(2,1)} %reshape.120), calls=%async_computation.1 | async-start | bytes 655360 | tf_op jit(solution)/shard_map/all_to_all | solution.py:74
  68.7 187.7 %all-gather.2.cloned.1.call-start = ((), (), s32[]{:S(2)}) async-start(), calls=%async_computation.2 | async-start | bytes 21626880 | tf_op jit(solution)/shard_map/all_gather | solution.py:89
  85.3 5.0 %copy-start.1 = (f32[1,8,32,640]{3,2,1,0:T(8,128)S(1)}, f32[1,8,32,640]{3,2,1,0:T(8,128)}, u32[]{:S(2)}) copy-start(f32[1,8,32,640]{3,2,1,0:T(8,128)} %param.5) | copy-start | bytes 1966084
  90.2 1.1 copy-start.3
  90.2 3.0 %copy-start.5 = (s32[32]{0:T(128)S(1)}, s32[32]{0:T(128)}, u32[]{:S(2)}) copy-start(s32[32]{0:T(128)} %param.9) | copy-start | bytes 388
Sparse Core Ops, SparseCore 0:
  91.5 164.8 all-gather.1
where the time goes:
time: 274 us
  waiting for transfers between devices  150 us (55%)
  local copies, waits for them, and re-layouts  30.6 us (11%)
  other arithmetic  24.6 us (9%)
  blocking collectives  23.4 us (9%)
  between operations  17.8 us (6%)
  starting transfers between devices  14.7 us (5%)
  matrix products  12.9 us (5%)
    all_gather x1, waiting for transfers between devices, on_device(): shards = lax.all_gather(stepped, 'member', axis=0, tiled=True)  131 us
    psum x1, blocking collectives, on_device(): region_total = lax.psum(region_part, 'wave')  23.4 us
    unnamed x16, local copies, waits for them, and re-layouts  17.9 us
    all_to_all x1, waiting for transfers between devices, on_device(): lax.all_to_all(flux_coef, 'wave', split_axis=0, concat_axis=3, tiled=True)  12.8 us
    all_to_all x1, starting transfers between devices, on_device(): lax.all_to_all(fourier_coef, 'wave', split_axis=3, concat_axis=0, tiled=T...  10.8 us
    reduce_sum x1, other arithmetic, on_device(): jnp.sum(jnp.where(owners == source_member, shards, 0.0), axis=0, keepdims...  9.6 us
    all_to_all x1, waiting for transfers between devices, on_device(): lax.all_to_all(fourier_coef, 'wave', split_axis=3, concat_axis=0, tiled=T...  6.27 us
    another operation x1, other arithmetic  6.15 us
  transfers between devices with their start and end apart: 3, of which 3 were waited for; matrix products, arithmetic and copies ran while one was open for 5% of the time, Pallas kernels for 0%

commit v1 on v0

--- a/solution.py
+++ b/solution.py
@@ -86,7 +86,8 @@
     imag_part = (spectral_split[:, 1] - advection * tendency[:, 0]) / damping
     stepped = jnp.stack([real_part, imag_part], axis=1).reshape(1, waves_local, state_rows, degrees)
     source_member = sources[lax.axis_index("member")]
-    shards = lax.all_gather(stepped, "member", axis=0, tiled=True)
+    sent = jnp.stack([stepped] * lax.axis_size("member"))
+    shards = jnp.concatenate(lax.all_to_all(sent, "member", 0, 0), axis=0)
     owners = lax.broadcasted_iota(jnp.int32, (shards.shape[0], 1, 1, 1), 0)
     cloned = jnp.sum(jnp.where(owners == source_member, shards, 0.0), axis=0, keepdims=True)
     return (cloned, scores)

time: 274 us -> 639 us (2.33)
  the two profiles are of different devices: /device:TPU:1 before, /device:TPU:136 now
where the time goes in v1:
time: 639 us; the launch traced here: 638 us
  waiting for transfers between devices  509 us (80%)
  local copies, waits for them, and re-layouts  40.2 us (6%)
  starting transfers between devices  24.7 us (4%)
  blocking collectives  23.8 us (4%)
  other arithmetic  23.7 us (4%)
  matrix products  12.9 us (2%)
    all_to_all x1, waiting for transfers between devices, on_device(): shards = jnp.concatenate(lax.all_to_all(sent, 'member', 0, 0), axis=0)  493 us
    psum x1, blocking collectives, on_device(): region_total = lax.psum(region_part, 'wave')  23.8 us
    unnamed x16, local copies, waits for them, and re-layouts  17.9 us
  transfers between devices with their start and end apart: 3, of which 3 were waited for; matrix products, arithmetic and copies ran while one was open for 2% of the time, Pallas kernels for 0%

profile of v1, /device:TPU:136, one launch (start us, length us, event | category | flops | bytes accessed | tf_op | source)
XLA Modules:
  0.0 638.4 jit_solution(7231766719573247531)
XLA Ops:
  0.6 4.2 convolution_convert_fusion
  4.8 3.3 copy.16
  8.1 3.4 reshape.122
  11.6 7.6 %all-to-all-start = ((bf16[16,2,5120]{2,1,0:T(2,128)(2,1)}), bf16[16,2,5120]{2,1,0:T(2,128)(2,1)}, u32[]{:S(2)}, u32[]{:S(2)}) async-start(bf16[16,2,5120]{2,1,0:T(2,128)(2,1)} %reshape.122), calls=%async_computation | async-start | bytes 655360 | tf_op jit(solution)/shard_map/all_to_all | solution.py:37
  19.2 6.1 negate_convert_fusion
  25.4 4.6 all-to-all-done
  29.9 8.5 %reshape.123 = bf16[640,8,2,16]{3,2,1,0:T(2,128)(2,1)S(1)} reshape(bf16[16,2,5120]{2,1,0:T(2,128)(2,1)} %all-to-all-done) | data formatting | bytes 655360
  38.5 4.7 copy.27
  43.2 2.5 bitcast_multiply_fusion
  45.7 0.8 multiply_multiply_fusion
  46.6 1.9 copy-done
  48.5 1.2 fusion.19
  49.7 1.4 copy.20
  51.2 2.4 reshape.124
  53.6 5.3 all-to-all-start.1
  58.9 11.1 %all-to-all-done.1 = bf16[16,2,5120]{2,1,0:T(2,128)(2,1)S(1)} async-done(((bf16[16,2,5120]{2,1,0:T(2,128)(2,1)}), bf16[16,2,5120]{2,1,0:T(2,128)(2,1)S(1)}, u32[]{:S(2)}, u32[]{:S(2)}) %all-to-all-start.1) | async-done | bytes 327712 | tf_op jit(solution)/shard_map/all_to_all | solution.py:74
  70.0 1.6 reshape.125
  71.6 0.7 copy.21
  72.3 1.2 all_to_all.36
  73.5 4.9 fusion.2
  78.7 9.6 %stack.16 = f32[32,1,8,32,640]{4,3,2,1,0:T(8,128)} broadcast(f32[8,32,640]{2,1,0:T(8,128)S(1)} %bitcast.68), dimensions={2,3,4} | broadcast | bytes 21626880 | tf_op jit(solution)/shard_map/stack | solution.py:89
  88.3 11.9 %all-to-all-start.2 = ((f32[32,1,8,32,640]{4,3,2,1,0:T(8,128)}), f32[32,1,8,32,640]{4,3,2,1,0:T(8,128)}, u32[]{:S(2)}, u32[]{:S(2)}) async-start(f32[32,1,8,32,640]{4,3,2,1,0:T(8,128)} %stack.16), calls=%async_computation.2 | async-start | bytes 41943040 | tf_op jit(solution)/shard_map/all_to_all | solution.py:90
  100.2 0.7 fusion.37
  102.0 0.6 dynamic_slice.6
  102.6 0.6 iota_compare_fusion.4
  103.3 1.3 compare_and_fusion
  104.6 1.1 iota_compare_fusion
  105.7 1.9 select_reduce_fusion
  107.7 1.9 fusion.26
  110.1 23.8 %psum.7 = f32[]{:T(128)} all-reduce(f32[]{:T(128)} %fusion.26), channel_id=1, replica_groups=mesh['member'=32,'wave'=16] {'wave'}, use_global_device_ids=true, to_apply=%region_2.3 | all-reduce | flops 1 | bytes 8 | tf_op jit(solution)/shard_map/psum | solution.py:60
  134.6 493.1 %all-to-all-done.2 = f32[32,1,8,32,640]{4,3,2,1,0:T(8,128)} async-done(((f32[32,1,8,32,640]{4,3,2,1,0:T(8,128)}), f32[32,1,8,32,640]{4,3,2,1,0:T(8,128)}, u32[]{:S(2)}, u32[]{:S(2)}) %all-to-all-start.2) | async-done | bytes 20971552 | tf_op jit(solution)/shard_map/all_to_all | solution.py:90
  627.7 9.6 %fusion = f32[8,32,640]{2,1,0:T(8,128)} fusion(f32[32,1,8,32,640]{4,3,2,1,0:T(8,128)} %all-to-all-done.2, pred[32]{0:T(512)(128)(4,1)S(1)} %iota_compare_fusion.4), kind=kLoop, calls=%fused_computation.1 | loop fusion | flops 10321920 | bytes 21626912 | tf_op jit(solution)/shard_map/reduce_sum | solution.py:92
  (16 shorter events, 0.3 us)
Async XLA Ops:
  4.8 14.3 %copy-start.4 = (f32[640]{0:T(1024)S(1)}, f32[640]{0:T(1024)}, u32[]{:S(2)}) copy-start(f32[640]{0:T(1024)} %param.7) | copy-start | bytes 7684
  11.6 18.4 %all-to-all-start = ((bf16[16,2,5120]{2,1,0:T(2,128)(2,1)}), bf16[16,2,5120]{2,1,0:T(2,128)(2,1)}, u32[]{:S(2)}, u32[]{:S(2)}) async-start(bf16[16,2,5120]{2,1,0:T(2,128)(2,1)} %reshape.122), calls=%async_computation | async-start | bytes 655360 | tf_op jit(solution)/shard_map/all_to_all | solution.py:37
  45.7 2.8 copy-start
  45.7 2.8 copy-start.2
  53.6 16.4 %all-to-all-start.1 = ((bf16[16,2,5120]{2,1,0:T(2,128)(2,1)}), bf16[16,2,5120]{2,1,0:T(2,128)(2,1)S(1)}, u32[]{:S(2)}, u32[]{:S(2)}) async-start(bf16[16,2,5120]{2,1,0:T(2,128)(2,1)} %reshape.124), calls=%async_computation.1 | async-start | bytes 655360 | tf_op jit(solution)/shard_map/all_to_all | solution.py:74
  73.5 5.0 copy-start.1
  88.3 11.9 %copy-start.3 = (s32[4]{0:T(128)S(1)}, s32[4]{0:T(128)}, u32[]{:S(2)}) copy-start(s32[4]{0:T(128)} %param.8) | copy-start | bytes 52
  88.3 13.7 %copy-start.5 = (s32[32]{0:T(128)S(1)}, s32[32]{0:T(128)}, u32[]{:S(2)}) copy-start(s32[32]{0:T(128)} %param.9) | copy-start | bytes 388
  88.3 539.3 %all-to-all-start.2 = ((f32[32,1,8,32,640]{4,3,2,1,0:T(8,128)}), f32[32,1,8,32,640]{4,3,2,1,0:T(8,128)}, u32[]{:S(2)}, u32[]{:S(2)}) async-start(f32[32,1,8,32,640]{4,3,2,1,0:T(8,128)} %stack.16), calls=%async_computation.2 | async-start | bytes 41943040 | tf_op jit(solution)/shard_map/all_to_all | solution.py:90
